TPU v7x, 32 devices: a whole 2x2x4 slice. The times are simulated.
32 devices in a mesh: grp: 8 (over z, core), tp: 4 (over y, x).
Axes of the slice: x: 2, y: 2, z: 4, core: 2. Of those that a mesh axis runs over, the one named last changes fastest.
Arguments:
- hidden: bfloat16 [128, 16384], P(('grp', 'tp')), may hold values from -130 to 130
- gain: float32 [16384], replicated, may hold values from 0.5 to 1.5
- head: bfloat16 [16384, 16384], P(None, ('grp', 'tp')), may hold values from -3 to 3
Outputs:
- log_probs: float32 [128, 16384], P(('grp', 'tp'))
All inputs are finite; a program needn't handle non-finite values.
Results may differ from a plain program's by a relative error of at most 0.00055.
Values may be sent and summed in bfloat16 or wider, within the bound.
No kernel may reach another device: no remote copies, remote signals or barrier semaphores. Data moves between devices by JAX's collectives and lax.ppermute only.
A program may use at most 128 MiB of HBM per device.

v0:
```python
import jax
import jax.numpy as jnp
from jax import lax
from jax.sharding import PartitionSpec as P


def on_device(hidden, gain, head):
    values = hidden.astype(jnp.float32)
    mean_square = jnp.mean(values * values, axis=-1, keepdims=True)
    normed = (values * lax.rsqrt(mean_square + 1e-05) * gain).astype(jnp.bfloat16)
    group_block = lax.all_gather(normed, "tp", axis=0, tiled=True)
    logits = jnp.dot(
        lax.all_gather(group_block, "grp", axis=0, tiled=True),
        head,
        preferred_element_type=jnp.float32,
    )
    owned = lax.all_to_all(logits, ("grp", "tp"), split_axis=0, concat_axis=1, tiled=True)
    top = jnp.max(owned, axis=-1, keepdims=True)
    total = jnp.sum(jnp.exp(owned - top), axis=-1, keepdims=True)
    return owned - top - jnp.log(total)


def solution(mesh):
    return jax.shard_map(
        on_device,
        mesh=mesh,
        in_specs=(P(("grp", "tp"), None), P(), P(None, ("grp", "tp"))),
        out_specs=P(("grp", "tp"), None),
        check_vma=False,
    )
```

profile of v0, /device:TPU:0, one launch (start us, length us, event | category | flops | bytes accessed | tf_op | source)
XLA Modules:
  0.0 100.4 jit_solution(16595028020233734949)
XLA Ops:
  6.5 0.0 all-gather.3.cloned.1.call-start
  6.5 1.2 %fusion = f32[4]{0:T(128)S(1)} fusion(bf16[4,16384]{1,0:T(4,128)(2,1)} %param.3), kind=kLoop, calls=%fused_computation.2 | loop fusion | flops 196604 | bytes 131088 | tf_op jit(solution)/shard_map/reduce_sum | solution.py:9
  7.7 1.0 %fusion.5 = bf16[1,4,16384]{2,1,0:T(4,128)(2,1)S(1)} fusion(bf16[4,16384]{1,0:T(4,128)(2,1)} %param.3, f32[16384]{0:T(1024)} %param.4, f32[4]{0:T(128)S(1)} %add_rsqrt_fusion), kind=kLoop, calls=%fused_computation.9 | loop fusion | flops 262144 | bytes 327696
  8.7 11.5 %all-gather = bf16[4,4,16384]{2,1,0:T(4,128)(2,1)S(1)} all-gather(bf16[1,4,16384]{2,1,0:T(4,128)(2,1)S(1)} %fusion.5), channel_id=1, replica_groups=mesh['grp'=8,'tp'=4] {'tp'}, dimensions={0}, use_global_device_ids=true | all-gather | bytes 655360 | tf_op jit(solution)/shard_map/all_gather | solution.py:11
  20.3 0.9 reshape.22
  21.2 0.0 all-gather.3.cloned.1.call-update
  21.2 47.3 %all-gather.3.cloned.1.call-done = bf16[128,16384]{1,0:T(8,128)(2,1)} async-done(((bf16[16,16384]{1,0:T(8,128)(2,1)}), bf16[128,16384]{1,0:T(8,128)(2,1)}) %all-gather.3.cloned.1.call-update) | async-done | bytes 4194320 | tf_op jit(solution)/shard_map/all_gather | solution.py:13
  68.5 9.4 %fusion.6 = f32[128,512]{1,0:T(8,128)S(1)} fusion(bf16[128,16384]{1,0:T(8,128)(2,1)} %all-gather.3.cloned.1.call-done, bf16[16384,512]{1,0:T(8,128)(2,1)} %param.5), kind=kOutput, calls=%fused_computation.11 | convolution fusion | flops 2147483648 | bytes 21233664 | tf_op jit(solution)/shard_map/dot_general | solution.py:12
  77.9 0.1 all_to_all.14
  78.0 14.1 %all_to_all.19 = f32[32,4,512]{2,1,0:T(4,128)S(1)} all-to-all(f32[32,4,512]{2,1,0:T(4,128)S(1)} %all_to_all.14), channel_id=1, replica_groups=mesh['grp'=8,'tp'=4] {'grp','tp'}, dimensions={0} | all-to-all | bytes 524288 | tf_op jit(solution)/shard_map/all_to_all | solution.py:17
  92.1 0.3 reduce_max.9
  92.4 0.3 fusion.4
  92.7 0.8 subtract_subtract_fusion
  (2 shorter events, 0.0 us)
Async XLA Ops:
  6.5 62.0 %all-gather.3.cloned.1.call-start = ((), (), s32[]{:S(2)}) async-start(), calls=%async_computation.1 | async-start | bytes 4718592 | tf_op jit(solution)/shard_map/all_gather | solution.py:13
Sparse Core Ops, SparseCore 0:
  21.3 47.1 all-gather.2
where the time goes:
time: 101 us; the launch traced here: 100 us
  waiting for transfers between devices  47.3 us (47%)
  blocking collectives  25.7 us (25%)
  between operations  13.4 us (13%)
  matrix products  9.38 us (9%)
  other arithmetic  3.61 us (4%)
    all_gather x1, waiting for transfers between devices, on_device(): lax.all_gather(group_block, 'grp', axis=0, tiled=True)  47.3 us
    all_to_all x1, blocking collectives, on_device(): lax.all_to_all(logits, ('grp', 'tp'), split_axis=0, concat_axis=1, tiled=...  14.1 us
    all_gather x1, blocking collectives, on_device(): group_block = lax.all_gather(normed, 'tp', axis=0, tiled=True)  11.5 us
    dot_general x1, matrix products, on_device(): jnp.dot(lax.all_gather(group_block, 'grp', axis=0, tiled=True), head, pre...  9.38 us
  transfers between devices with their start and end apart: 1, of which 1 were waited for; matrix products, arithmetic and copies ran while one was open for 0% of the time, Pallas kernels for 0%

commit v1 on v0

--- a/solution.py
+++ b/solution.py
@@ -14,7 +14,9 @@
         head,
         preferred_element_type=jnp.float32,
     )
-    owned = lax.all_to_all(logits, ("grp", "tp"), split_axis=0, concat_axis=1, tiled=True)
+    pieces = jnp.split(logits, lax.axis_size(("grp", "tp")), axis=0)
+    got = lax.all_to_all(jnp.stack(pieces), ("grp", "tp"), 0, 0)
+    owned = jnp.concatenate(got, axis=1)
     top = jnp.max(owned, axis=-1, keepdims=True)
     total = jnp.sum(jnp.exp(owned - top), axis=-1, keepdims=True)
     return owned - top - jnp.log(total)

time: 101 us -> 101 us (level)
  no operation moved by 1% of the time
where the time goes in v1:
time: 101 us
  waiting for transfers between devices  47.3 us (47%)
  blocking collectives  25.7 us (25%)
  between operations  13.5 us (13%)
  matrix products  9.38 us (9%)
  other arithmetic  3.61 us (4%)
  local copies, waits for them, and re-layouts  1.25 us (1%)
    all_gather x1, waiting for transfers between devices, on_device(): lax.all_gather(group_block, 'grp', axis=0, tiled=True)  47.3 us
    all_to_all x1, blocking collectives, on_device(): got = lax.all_to_all(jnp.stack(pieces), ('grp', 'tp'), 0, 0)  14.1 us
    all_gather x1, blocking collectives, on_device(): group_block = lax.all_gather(normed, 'tp', axis=0, tiled=True)  11.5 us
    dot_general x1, matrix products, on_device(): jnp.dot(lax.all_gather(group_block, 'grp', axis=0, tiled=True), head, pre...  9.38 us
  transfers between devices with their start and end apart: 1, of which 1 were waited for; matrix products, arithmetic and copies ran while one was open for 0% of the time, Pallas kernels for 0%

profile of v1, /device:TPU:0, one launch (start us, length us, event | category | flops | bytes accessed | tf_op | source)
XLA Modules:
  0.0 100.8 jit_solution(1186990782019695218)
XLA Ops:
  6.5 0.0 all-gather.3.cloned.1.call-start
  6.5 1.2 %fusion = f32[4]{0:T(128)S(1)} fusion(bf16[4,16384]{1,0:T(4,128)(2,1)} %param.3), kind=kLoop, calls=%fused_computation.2 | loop fusion | flops 196604 | bytes 131088 | tf_op jit(solution)/shard_map/reduce_sum | solution.py:9
  7.7 1.0 %fusion.5 = bf16[1,4,16384]{2,1,0:T(4,128)(2,1)S(1)} fusion(bf16[4,16384]{1,0:T(4,128)(2,1)} %param.3, f32[16384]{0:T(1024)} %param.4, f32[4]{0:T(128)S(1)} %add_rsqrt_fusion), kind=kLoop, calls=%fused_computation.9 | loop fusion | flops 262144 | bytes 327696
  8.7 11.5 %all-gather = bf16[4,4,16384]{2,1,0:T(4,128)(2,1)S(1)} all-gather(bf16[1,4,16384]{2,1,0:T(4,128)(2,1)S(1)} %fusion.5), channel_id=1, replica_groups=mesh['grp'=8,'tp'=4] {'tp'}, dimensions={0}, use_global_device_ids=true | all-gather | bytes 655360 | tf_op jit(solution)/shard_map/all_gather | solution.py:11
  20.3 0.9 reshape.27
  21.2 0.0 all-gather.3.cloned.1.call-update
  21.2 47.3 %all-gather.3.cloned.1.call-done = bf16[128,16384]{1,0:T(8,128)(2,1)} async-done(((bf16[16,16384]{1,0:T(8,128)(2,1)}), bf16[128,16384]{1,0:T(8,128)(2,1)}) %all-gather.3.cloned.1.call-update) | async-done | bytes 4194320 | tf_op jit(solution)/shard_map/all_gather | solution.py:13
  68.5 9.4 %fusion.6 = f32[128,512]{1,0:T(8,128)S(1)} fusion(bf16[128,16384]{1,0:T(8,128)(2,1)} %all-gather.3.cloned.1.call-done, bf16[16384,512]{1,0:T(8,128)(2,1)} %param.5), kind=kOutput, calls=%fused_computation.75 | convolution fusion | flops 2147483648 | bytes 21233664 | tf_op jit(solution)/shard_map/dot_general | solution.py:12
  78.4 14.1 %all_to_all.5 = f32[32,4,512]{2,1,0:T(4,128)S(1)} all-to-all(f32[32,4,512]{2,1,0:T(4,128)S(1)} %constant_dynamic-update-slice_fusion), channel_id=1, replica_groups=mesh['grp'=8,'tp'=4] {'grp','tp'}, dimensions={0} | all-to-all | bytes 524288 | tf_op jit(solution)/shard_map/all_to_all | solution.py:18
  92.5 0.3 reduce_max.9
  92.7 0.3 fusion.4
  93.1 0.8 subtract_subtract_fusion
  (34 shorter events, 0.3 us)
Async XLA Ops:
  6.5 62.0 %all-gather.3.cloned.1.call-start = ((), (), s32[]{:S(2)}) async-start(), calls=%async_computation.1 | async-start | bytes 4718592 | tf_op jit(solution)/shard_map/all_gather | solution.py:13
Sparse Core Ops, SparseCore 0:
  21.3 47.1 all-gather.2

commit v2 on v0

--- a/solution.py
+++ b/solution.py
@@ -8,7 +8,13 @@
     values = hidden.astype(jnp.float32)
     mean_square = jnp.mean(values * values, axis=-1, keepdims=True)
     normed = (values * lax.rsqrt(mean_square + 1e-05) * gain).astype(jnp.bfloat16)
-    group_block = lax.all_gather(normed, "tp", axis=0, tiled=True)
+    size = lax.axis_size("tp")
+    moving, shards = (normed, [normed])
+    for _ in range(size - 1):
+        moving = lax.ppermute(moving, "tp", [(i, (i + 1) % size) for i in range(size)])
+        shards.insert(0, moving)
+    line = jnp.concatenate(shards, axis=0)
+    group_block = jnp.roll(line, (lax.axis_index("tp") + 1) * normed.shape[0], axis=0)
     logits = jnp.dot(
         lax.all_gather(group_block, "grp", axis=0, tiled=True),
         head,

time: 101 us -> 109 us (1.079)
  waiting for transfers between devices: 47.3 us -> 62.9 us
  blocking collectives: 25.7 us -> 14.1 us
  starting transfers between devices: 0.01 us -> 3.81 us
    ppermute x0 -> x3, waiting for transfers between devices: none -> 15.4 us  [on_device(): lax.ppermute(moving, 'tp', [(i, (i + 1) % size) for i in range(size)])]
    all_gather x1 -> x0, blocking collectives: 11.5 us -> none  [on_device(): group_block = lax.all_gather(normed, 'tp', axis=0, tiled=True)]
    ppermute x0 -> x3, starting transfers between devices: none -> 3.81 us  [on_device(): lax.ppermute(moving, 'tp', [(i, (i + 1) % size) for i in range(size)])]
  transfers between devices with their start and end apart: 1 -> 4, of which waited for: 1 -> 4; matrix products, arithmetic and copies ran while one was open for 0% -> 0% of each run, Pallas kernels for 0% -> 0%
where the time goes in v2:
time: 109 us
  waiting for transfers between devices  62.9 us (58%)
  blocking collectives  14.1 us (13%)
  between operations  13.4 us (12%)
  matrix products  9.38 us (9%)
  starting transfers between devices  3.81 us (3%)
  other arithmetic  3.61 us (3%)
  local copies, waits for them, and re-layouts  1.91 us (2%)
    all_gather x1, waiting for transfers between devices, on_device(): lax.all_gather(group_block, 'grp', axis=0, tiled=True)  47.5 us
    ppermute x3, waiting for transfers between devices, on_device(): lax.ppermute(moving, 'tp', [(i, (i + 1) % size) for i in range(size)])  15.4 us
    all_to_all x1, blocking collectives, on_device(): lax.all_to_all(logits, ('grp', 'tp'), split_axis=0, concat_axis=1, tiled=...  14.1 us
    dot_general x1, matrix products, on_device(): jnp.dot(lax.all_gather(group_block, 'grp', axis=0, tiled=True), head, pre...  9.38 us
    ppermute x3, starting transfers between devices, on_device(): lax.ppermute(moving, 'tp', [(i, (i + 1) % size) for i in range(size)])  3.81 us
  transfers between devices with their start and end apart: 4, of which 4 were waited for; matrix products, arithmetic and copies ran while one was open for 0% of the time, Pallas kernels for 0%

profile of v2, /device:TPU:0, one launch (start us, length us, event | category | flops | bytes accessed | tf_op | source)
XLA Modules:
  0.0 109.2 jit_solution(11134192929308538358)
XLA Ops:
  6.5 0.0 all-gather.2.cloned.1.call-start
  6.5 1.2 %fusion = f32[4]{0:T(128)S(1)} fusion(bf16[4,16384]{1,0:T(4,128)(2,1)} %param.3), kind=kLoop, calls=%fused_computation.2 | loop fusion | flops 196604 | bytes 131088 | tf_op jit(solution)/shard_map/reduce_sum | solution.py:9
  7.7 1.0 fusion.2
  8.7 3.0 %collective-permute-start = (bf16[4,16384]{1,0:T(4,128)(2,1)S(1)}, bf16[4,16384]{1,0:T(4,128)(2,1)S(1)}, u32[]{:S(2)}, u32[]{:S(2)}) collective-permute-start(bf16[4,16384]{1,0:T(4,128)(2,1)S(1)} %fusion.2), channel_id=1, source_target_pairs={{0,1},{1,2},{2,3},{3,0},{4,5},{5,6},{6,7},{7,4},{8,9},{9,10},{10,1... | collective-permute-start | bytes 393224 | tf_op jit(solution)/shard_map/ppermute | solution.py:14
  11.8 4.5 %collective-permute-done = bf16[4,16384]{1,0:T(4,128)(2,1)S(1)} collective-permute-done((bf16[4,16384]{1,0:T(4,128)(2,1)S(1)}, bf16[4,16384]{1,0:T(4,128)(2,1)S(1)}, u32[]{:S(2)}, u32[]{:S(2)}) %collective-permute-start) | collective-permute-done | bytes 131104 | tf_op jit(solution)/shard_map/ppermute | solution.py:14
  16.2 0.8 collective-permute-start.1
  17.0 5.1 %collective-permute-done.1 = bf16[4,16384]{1,0:T(4,128)(2,1)S(1)} collective-permute-done((bf16[4,16384]{1,0:T(4,128)(2,1)S(1)}, bf16[4,16384]{1,0:T(4,128)(2,1)S(1)}, u32[]{:S(2)}, u32[]{:S(2)}) %collective-permute-start.1) | collective-permute-done | bytes 131104 | tf_op jit(solution)/shard_map/ppermute | solution.py:14
  22.1 0.0 collective-permute-start.2
  22.1 5.9 %collective-permute-done.2 = bf16[4,16384]{1,0:T(4,128)(2,1)S(1)} collective-permute-done((bf16[4,16384]{1,0:T(4,128)(2,1)S(1)}, bf16[4,16384]{1,0:T(4,128)(2,1)S(1)}, u32[]{:S(2)}, u32[]{:S(2)}) %collective-permute-start.2) | collective-permute-done | bytes 131104 | tf_op jit(solution)/shard_map/ppermute | solution.py:14
  28.0 0.9 concatenate.6
  28.8 0.9 constant_dynamic-slice_fusion
  29.8 0.0 all-gather.2.cloned.1.call-update
  29.8 47.5 %all-gather.2.cloned.1.call-done = bf16[128,16384]{1,0:T(8,128)(2,1)} async-done(((bf16[16,16384]{1,0:T(8,128)(2,1)}), bf16[128,16384]{1,0:T(8,128)(2,1)}) %all-gather.2.cloned.1.call-update) | async-done | bytes 4194320 | tf_op jit(solution)/shard_map/all_gather | solution.py:19
  77.3 9.4 %fusion.5 = f32[128,512]{1,0:T(8,128)S(1)} fusion(bf16[128,16384]{1,0:T(8,128)(2,1)} %all-gather.2.cloned.1.call-done, bf16[16384,512]{1,0:T(8,128)(2,1)} %param.5), kind=kOutput, calls=%fused_computation.11 | convolution fusion | flops 2147483648 | bytes 21233664 | tf_op jit(solution)/shard_map/dot_general | solution.py:18
  86.7 0.1 all_to_all.14
  86.8 14.1 %all_to_all.19 = f32[32,4,512]{2,1,0:T(4,128)S(1)} all-to-all(f32[32,4,512]{2,1,0:T(4,128)S(1)} %all_to_all.14), channel_id=1, replica_groups=mesh['grp'=8,'tp'=4] {'grp','tp'}, dimensions={0} | all-to-all | bytes 524288 | tf_op jit(solution)/shard_map/all_to_all | solution.py:23
  101.0 0.3 reduce_max.9
  101.2 0.3 fusion.4
  101.5 0.8 subtract_subtract_fusion
  (2 shorter events, 0.0 us)
Async XLA Ops:
  6.5 70.8 %all-gather.2.cloned.1.call-start = ((), (), s32[]{:S(2)}) async-start(), calls=%async_computation.1 | async-start | bytes 4718592 | tf_op jit(solution)/shard_map/all_gather | solution.py:19
  8.7 7.5 %collective-permute-start = (bf16[4,16384]{1,0:T(4,128)(2,1)S(1)}, bf16[4,16384]{1,0:T(4,128)(2,1)S(1)}, u32[]{:S(2)}, u32[]{:S(2)}) collective-permute-start(bf16[4,16384]{1,0:T(4,128)(2,1)S(1)} %fusion.2), channel_id=1, source_target_pairs={{0,1},{1,2},{2,3},{3,0},{4,5},{5,6},{6,7},{7,4},{8,9},{9,10},{10,1... | collective-permute-start | bytes 393224 | tf_op jit(solution)/shard_map/ppermute | solution.py:14
  16.2 5.9 %collective-permute-start.1 = (bf16[4,16384]{1,0:T(4,128)(2,1)S(1)}, bf16[4,16384]{1,0:T(4,128)(2,1)S(1)}, u32[]{:S(2)}, u32[]{:S(2)}) collective-permute-start(bf16[4,16384]{1,0:T(4,128)(2,1)S(1)} %collective-permute-done), channel_id=1, source_target_pairs={{0,1},{1,2},{2,3},{3,0},{4,5},{5,6},{6,7},{7,4},{8,9},{9,10},{10,1... | collective-permute-start | bytes 393224 | tf_op jit(solution)/shard_map/ppermute | solution.py:14
  22.1 5.9 %collective-permute-start.2 = (bf16[4,16384]{1,0:T(4,128)(2,1)S(1)}, bf16[4,16384]{1,0:T(4,128)(2,1)S(1)}, u32[]{:S(2)}, u32[]{:S(2)}) collective-permute-start(bf16[4,16384]{1,0:T(4,128)(2,1)S(1)} %collective-permute-done.1), channel_id=1, source_target_pairs={{0,1},{1,2},{2,3},{3,0},{4,5},{5,6},{6,7},{7,4},{8,9},{9,10},{10,1... | collective-permute-start | bytes 393224 | tf_op jit(solution)/shard_map/ppermute | solution.py:14
Sparse Core Ops, SparseCore 0:
  29.9 47.3 all-gather.1
